TPU v7x, 32 devices: a whole 2x2x4 slice. The times are simulated.
32 devices in a mesh: dp: 2 (over y), tile: 4 (over z), replica: 4 (over x, core).
Axes of the slice: x: 2, y: 2, z: 4, core: 2. Of those that a mesh axis runs over, the one named last changes fastest.
Arguments:
- tokens: bfloat16 [128, 8192], P(('tile', 'replica'), 'dp'), may hold values from -6 to 6
- out_grad: bfloat16 [128, 8192], P(('tile', 'replica'), 'dp'), may hold values from -3 to 3
- gate_blocks: bfloat16 [2, 4, 384, 128, 128], P('dp', 'tile'), may hold values from -0.125 to 0.125
- up_blocks: bfloat16 [2, 4, 384, 128, 128], P('dp', 'tile'), may hold values from -0.125 to 0.125
- down_blocks: bfloat16 [2, 4, 384, 128, 128], P('dp', 'tile'), may hold values from -0.09375 to 0.09375
- gate_ids: int32 [2, 4, 384], P('dp', 'tile'), may hold values from 0 to 896, as said below
- up_ids: int32 [2, 4, 384], P('dp', 'tile'), may hold values from 0 to 896, as said below
- down_ids: int32 [2, 4, 384], P('dp', 'tile'), may hold values from 0 to 896, as said below
Outputs:
- output: bfloat16 [128, 8192], P(('tile', 'replica'), 'dp')
- input_grad: bfloat16 [128, 8192], P(('tile', 'replica'), 'dp')
- gate_grad: bfloat16 [2, 4, 384, 128, 128], P('dp', 'tile')
- up_grad: bfloat16 [2, 4, 384, 128, 128], P('dp', 'tile')
- down_grad: bfloat16 [2, 4, 384, 128, 128], P('dp', 'tile')
Inputs may be any that keep to these rules, and one draw needn't show every extreme that they name: `gate_ids`: entry s for device (d, t) names a kept block of its 32 x 28 grid as row * 28 + column, each block at most once for a device; the value 896 marks an empty slot. Every device keeps 64 to 384 blocks; in every draw some device fills all 384 slots and another keeps 64 blocks. `up_ids`: as for gate_ids, drawn apart. `down_ids`: as for gate_ids, drawn apart; the row names a model-width block, the column a hidden-unit block.
All inputs are finite; a program needn't handle non-finite values.
Results may differ from a plain program's by a relative error of at most 0.017.
Values may be sent and summed in bfloat16 or wider, within the bound.
No kernel may reach another device: no remote copies, remote signals or barrier semaphores. Data moves between devices by JAX's collectives and lax.ppermute only.
A program may use at most 256 MiB of HBM per device.

v0:
```python
import jax
import jax.numpy as jnp
from jax import lax
from jax.sharding import PartitionSpec as P

FF = 14336


def block_slots(slot_ids, row_count, col_count):
    present = slot_ids < row_count * col_count
    row_index = jnp.where(present, slot_ids // col_count, row_count)
    col_index = jnp.where(present, slot_ids % col_count, col_count)
    return (row_index, col_index)


def select_blocks(matrix, index, block_count, block_size):
    blocked = matrix.reshape(matrix.shape[0], block_count, block_size)
    return jnp.take(blocked, index, axis=1, mode="fill", fill_value=0)


def place_blocks(product, index, block_count, block_size):
    placed = jnp.zeros((product.shape[0], block_count, block_size), jnp.float32)
    placed = placed.at[:, index, :].add(product, mode="drop")
    return placed.reshape(product.shape[0], block_count * block_size)


def on_device(tokens, out_grad, gate_blocks, up_blocks, down_blocks, gate_ids, up_ids, down_ids):
    gate_local = gate_blocks[0, 0]
    up_local = up_blocks[0, 0]
    down_local = down_blocks[0, 0]
    block_size = gate_local.shape[-1]
    token_rows, grad_rows = (
        lax.all_gather(tokens, "tile", axis=0, tiled=True),
        lax.all_gather(out_grad, "tile", axis=0, tiled=True),
    )
    row_count = token_rows.shape[1] // block_size
    hidden_width = FF // lax.axis_size("tile")
    col_count = hidden_width // block_size
    gate_rowslot, gate_colslot = block_slots(gate_ids[0, 0], row_count, col_count)
    up_rowslot, up_colslot = block_slots(up_ids[0, 0], row_count, col_count)
    down_rowslot, down_colslot = block_slots(down_ids[0, 0], row_count, col_count)
    gate_input = select_blocks(token_rows, gate_rowslot, row_count, block_size)
    up_input = select_blocks(token_rows, up_rowslot, row_count, block_size)
    gate_piece = gate_input
    up_piece = up_input
    gate_product = jnp.einsum(
        "tsk,skf->tsf", gate_piece, gate_local, preferred_element_type=jnp.float32
    )
    up_product = jnp.einsum("tsk,skf->tsf", up_piece, up_local, preferred_element_type=jnp.float32)
    gate_up = lax.psum_scatter(
        jnp.concatenate(
            [
                place_blocks(gate_product, gate_colslot, col_count, block_size),
                place_blocks(up_product, up_colslot, col_count, block_size),
            ],
            axis=1,
        ).astype(jnp.bfloat16),
        "dp",
        scatter_dimension=0,
        tiled=True,
    ).astype(jnp.float32)
    gate_sum = gate_up[:, :hidden_width]
    up_sum = gate_up[:, hidden_width:]
    sigmoid = jax.nn.sigmoid(gate_sum)
    silu_gate = gate_sum * sigmoid
    hidden = (silu_gate * up_sum).astype(jnp.bfloat16)
    hidden_rows = lax.all_gather(hidden, "dp", axis=0, tiled=True)
    hidden_picked = select_blocks(hidden_rows, down_colslot, col_count, block_size)
    grad_picked = select_blocks(grad_rows, down_rowslot, row_count, block_size)
    down_product = jnp.einsum(
        "tsf,sfk->tsk", hidden_picked, down_local, preferred_element_type=jnp.float32
    )
    output = lax.psum_scatter(
        place_blocks(down_product, down_rowslot, row_count, block_size).astype(jnp.bfloat16),
        "tile",
        scatter_dimension=0,
        tiled=True,
    )
    down_part = jnp.einsum(
        "tsf,tsk->sfk", hidden_picked, grad_picked, preferred_element_type=jnp.float32
    )
    back_product = jnp.einsum(
        "tsk,sfk->tsf", grad_picked, down_local, preferred_element_type=jnp.float32
    )
    hidden_grad = lax.psum_scatter(
        place_blocks(back_product, down_colslot, col_count, block_size).astype(jnp.bfloat16),
        "dp",
        scatter_dimension=0,
        tiled=True,
    ).astype(jnp.float32)
    gate_act_grad = (hidden_grad * up_sum * sigmoid * (1.0 + gate_sum * (1.0 - sigmoid))).astype(
        jnp.bfloat16
    )
    up_act_grad = (hidden_grad * silu_gate).astype(jnp.bfloat16)
    gate_grad_rows, up_grad_rows = (
        lax.all_gather(gate_act_grad, "dp", axis=0, tiled=True),
        lax.all_gather(up_act_grad, "dp", axis=0, tiled=True),
    )
    gate_grad_picked = select_blocks(gate_grad_rows, gate_colslot, col_count, block_size)
    up_grad_picked = select_blocks(up_grad_rows, up_colslot, col_count, block_size)
    gate_piece = gate_grad_picked
    up_piece = up_grad_picked
    gate_product = jnp.einsum(
        "tsf,skf->tsk", gate_piece, gate_local, preferred_element_type=jnp.float32
    )
    up_product = jnp.einsum("tsf,skf->tsk", up_piece, up_local, preferred_element_type=jnp.float32)
    input_grad = lax.psum_scatter(
        (
            place_blocks(gate_product, gate_rowslot, row_count, block_size)
            + place_blocks(up_product, up_rowslot, row_count, block_size)
        ).astype(jnp.bfloat16),
        "tile",
        scatter_dimension=0,
        tiled=True,
    )
    gate_part = jnp.einsum(
        "tsk,tsf->skf", gate_input, gate_grad_picked, preferred_element_type=jnp.float32
    )
    up_part = jnp.einsum(
        "tsk,tsf->skf", up_input, up_grad_picked, preferred_element_type=jnp.float32
    )
    gate_weight_grad, up_weight_grad, down_weight_grad = (
        lax.psum(gate_part.astype(jnp.bfloat16), "replica").astype(jnp.float32),
        lax.psum(up_part.astype(jnp.bfloat16), "replica").astype(jnp.float32),
        lax.psum(down_part.astype(jnp.bfloat16), "replica").astype(jnp.float32),
    )
    return (
        output,
        input_grad,
        gate_weight_grad.astype(jnp.bfloat16)[None, None],
        up_weight_grad.astype(jnp.bfloat16)[None, None],
        down_weight_grad.astype(jnp.bfloat16)[None, None],
    )


def solution(mesh):
    return jax.shard_map(
        on_device,
        mesh=mesh,
        in_specs=(
            P(("tile", "replica"), "dp"),
            P(("tile", "replica"), "dp"),
            P("dp", "tile", None, None, None),
            P("dp", "tile", None, None, None),
            P("dp", "tile", None, None, None),
            P("dp", "tile", None),
            P("dp", "tile", None),
            P("dp", "tile", None),
        ),
        out_specs=(
            P(("tile", "replica"), "dp"),
            P(("tile", "replica"), "dp"),
            P("dp", "tile", None, None, None),
            P("dp", "tile", None, None, None),
            P("dp", "tile", None, None, None),
        ),
        check_vma=False,
    )
```

profile of v0, /device:TPU:0, one launch (start us, length us, event | category | flops | bytes accessed | tf_op | source)
XLA Modules:
  0.0 1076.4 jit_solution(11249457878538878458)
XLA Ops:
  11.6 15.8 %all_gather.15 = bf16[32,4096]{1,0:T(8,128)(2,1)S(1)} all-gather(bf16[8,4096]{1,0:T(8,128)(2,1)} %param.12), channel_id=1, replica_groups=mesh['dp'=2,'tile'=4,'replica'=4] {'tile'}, dimensions={0}, use_global_device_ids=true | all-gather | bytes 327680 | tf_op jit(solution)/shard_map/all_gather | solution.py:33
  33.1 9.2 fusion.10
  42.4 34.9 %scatter_fusion = f32[32,28,128]{2,0,1:T(8,128)S(1)} fusion(f32[32,28,128]{2,0,1:T(8,128)S(1)} %broadcast.390.clone.2, s32[384]{0:T(512)S(1)} %get-tuple-element.14, f32[384,32,128]{2,1,0:T(8,128)} %fusion.10), kind=kCustom, calls=%fused_computation.6 | custom fusion | flops 1572864 | bytes 18875904 | tf_op jit(solution)/shard_map/scatter-add | solution.py:23
  77.3 11.7 %fusion.6 = f32[384,32,128]{2,1,0:T(8,128)} fusion(bf16[1,1,384,128,128]{4,3,2,1,0:T(8,128)(2,1)} %param.15, bf16[384,32,128]{2,1,0:T(8,128)(2,1)} %gather_fusion.1, pred[384]{0:T(512)(128)(4,1)S(1)} %get-tuple-element.43), kind=kOutput, calls=%fused_computation.18 | convolution fusion | flops 404226048 | bytes 22020480 | tf_op jit(solution)/shard_map/tsk,skf->tsf/dot_general | solution.py:49
  89.1 34.8 %scatter_fusion.1 = f32[32,28,128]{2,0,1:T(8,128)S(1)} fusion(f32[32,28,128]{2,0,1:T(8,128)S(1)} %broadcast.390.clone.1, s32[384]{0:T(512)S(1)} %get-tuple-element.8, f32[384,32,128]{2,1,0:T(8,128)} %fusion.6), kind=kCustom, calls=%fused_computation.7 | custom fusion | flops 1572864 | bytes 18875904 | tf_op jit(solution)/shard_map/scatter-add | solution.py:23
  124.9 14.7 %all_gather.17 = bf16[32,4096]{1,0:T(8,128)(2,1)S(1)} all-gather(bf16[8,4096]{1,0:T(8,128)(2,1)S(1)} %copy-done.6), channel_id=1, replica_groups=mesh['dp'=2,'tile'=4,'replica'=4] {'tile'}, dimensions={0}, use_global_device_ids=true | all-gather | bytes 327680 | tf_op jit(solution)/shard_map/all_gather | solution.py:34
  142.1 12.5 %fusion = f32[384,32,128]{2,1,0:T(8,128)} fusion(bf16[1,1,384,128,128]{4,3,2,1,0:T(8,128)(2,1)} %param.16, bf16[384,32,128]{2,1,0:T(8,128)(2,1)S(1)} %gather_fusion.3, pred[384]{0:T(512)(128)(4,1)S(1)} %get-tuple-element.26), kind=kOutput, calls=%fused_computation.12 | convolution fusion | flops 404226048 | bytes 22020480 | tf_op jit(solution)/shard_map/tsk,sfk->tsf/dot_general | solution.py:82
  154.7 34.9 %scatter_fusion.3 = f32[32,28,128]{2,0,1:T(8,128)S(1)} fusion(f32[32,28,128]{2,0,1:T(8,128)S(1)} %broadcast.390.clone, s32[384]{0:T(512)S(1)} %get-tuple-element.11, f32[384,32,128]{2,1,0:T(8,128)} %fusion), kind=kCustom, calls=%fused_computation.9 | custom fusion | flops 1572864 | bytes 18875904 | tf_op jit(solution)/shard_map/scatter-add | solution.py:23
  191.4 10.4 reduce-scatter.9.cloned.1.call-done
  202.9 5.6 all_gather.19
  211.7 15.1 %fusion.4 = f32[384,32,128]{2,1,0:T(8,128)} fusion(bf16[1,1,384,128,128]{4,3,2,1,0:T(8,128)(2,1)} %param.15, bf16[384,32,128]{2,1,0:T(8,128)(2,1)} %gather_fusion.5, pred[384]{0:T(512)(128)(4,1)S(1)} %get-tuple-element.22), kind=kOutput, calls=%fused_computation.16 | convolution fusion | flops 404226048 | bytes 22020480 | tf_op jit(solution)/shard_map/tsf,skf->tsk/dot_general | solution.py:106
  226.8 9.8 convert_bitcast_fusion.1
  242.1 5.6 all_gather.16
  251.0 14.9 %fusion.8 = f32[384,32,128]{2,1,0:T(8,128)} fusion(bf16[1,1,384,128,128]{4,3,2,1,0:T(8,128)(2,1)} %param.14, bf16[384,32,128]{2,1,0:T(8,128)(2,1)} %gather_fusion.4, pred[384]{0:T(512)(128)(4,1)S(1)} %get-tuple-element.24), kind=kOutput, calls=%fused_computation.20 | convolution fusion | flops 404226048 | bytes 22020480 | tf_op jit(solution)/shard_map/tsf,skf->tsk/dot_general | solution.py:103
  266.0 34.8 %scatter_fusion.5 = f32[32,32,128]{2,0,1:T(8,128)S(1)} fusion(f32[32,32,128]{2,0,1:T(8,128)S(1)} %broadcast.388.clone.2, s32[384]{0:T(512)S(1)} %get-tuple-element.7, f32[384,32,128]{2,1,0:T(8,128)} %fusion.4), kind=kCustom, calls=%fused_computation.11 | custom fusion | flops 1572864 | bytes 18875904 | tf_op jit(solution)/shard_map/scatter-add | solution.py:23
  300.9 34.9 %scatter_fusion.4 = f32[32,32,128]{2,0,1:T(8,128)S(1)} fusion(f32[32,32,128]{2,0,1:T(8,128)S(1)} %broadcast.388.clone.1, s32[384]{0:T(512)S(1)} %get-tuple-element.13, f32[384,32,128]{2,1,0:T(8,128)} %fusion.8), kind=kCustom, calls=%fused_computation.10 | custom fusion | flops 1572864 | bytes 18875904 | tf_op jit(solution)/shard_map/scatter-add | solution.py:23
  339.3 9.3 fusion.2
  348.6 34.9 %scatter_fusion.2 = f32[32,32,128]{2,0,1:T(8,128)S(1)} fusion(f32[32,32,128]{2,0,1:T(8,128)S(1)} %broadcast.388.clone, s32[384]{0:T(512)S(1)} %get-tuple-element.12, f32[384,32,128]{2,1,0:T(8,128)} %fusion.2), kind=kCustom, calls=%fused_computation.8 | custom fusion | flops 1572864 | bytes 18875904 | tf_op jit(solution)/shard_map/scatter-add | solution.py:23
  384.2 10.4 convert_bitcast_fusion.2
  394.8 9.8 convert_bitcast_fusion
  404.6 9.0 reduce-scatter.7.cloned.1.call-done
  413.6 630.0 %all-reduce.3.cloned.1.call-done = (bf16[1,1,384,128,128]{4,3,2,1,0:T(8,128)(2,1)}, bf16[1,1,384,128,128]{4,3,2,1,0:T(8,128)(2,1)}, bf16[1,1,384,128,128]{4,3,2,1,0:T(8,128)(2,1)}) async-done(((bf16[1,1,384,128,128]{4,3,2,1,0:T(8,128)(2,1)}, bf16[1,1,384,128,128]{4,3,2,1,0:T(8,128)(2,1)}, bf16[1,1,384,128,128]{4,3,2,1,0:T(8,128)(2,1)}), (bf16[1,1,384,128,128]{4,3,2,1,0:T(8,128)(2,1)}, ...) | async-done | bytes 37748752 | tf_op jit(solution)/shard_map/psum | solution.py:123
  1043.7 12.6 %copy.61 = bf16[1,1,384,128,128]{4,3,2,1,0:T(8,128)(2,1)} copy(bf16[1,1,384,128,128]{4,3,2,1,0:T(8,128)(2,1)} %get-tuple-element.57) | data formatting | bytes 25165824
  1056.3 6.4 copy.62
  (79 shorter events, 39.9 us)
Async XLA Ops:
  7.2 183.3 %reduce-scatter.5.cloned.1.call-start = ((), (), s32[]{:S(2)}) async-start(), calls=%async_computation.4 | async-start | bytes 688128 | tf_op jit(solution)/shard_map/reduce_scatter | solution.py:50
  33.1 9.2 copy-start
  89.1 35.8 %copy-start.7 = (s32[1,1,384]{2,1,0:T(1,128)S(1)}, s32[1,1,384]{2,1,0:T(1,128)}, u32[]{:S(2)}) copy-start(s32[1,1,384]{2,1,0:T(1,128)} %param.19) | copy-start | bytes 4612
  89.1 35.8 %copy-start.6 = (bf16[8,4096]{1,0:T(8,128)(2,1)S(1)}, bf16[8,4096]{1,0:T(8,128)(2,1)}, u32[]{:S(2)}) copy-start(bf16[8,4096]{1,0:T(8,128)(2,1)} %param.13) | copy-start | bytes 196612
  124.8 77.1 %reduce-scatter.9.cloned.1.call-start = ((), (), s32[]{:S(2)}) async-start(), calls=%async_computation.6 | async-start | bytes 344064 | tf_op jit(solution)/shard_map/reduce_scatter | solution.py:85
  142.1 12.5 %copy-start.4 = (bf16[384,32,128]{2,1,0:T(8,128)(2,1)}, bf16[384,32,128]{2,1,0:T(8,128)(2,1)S(1)}, u32[]{:S(2)}) copy-start(bf16[384,32,128]{2,1,0:T(8,128)(2,1)S(1)} %gather_fusion.3) | copy-start | bytes 9437188
  190.3 214.3 %reduce-scatter.11.cloned.1.call-start = ((), (), s32[]{:S(2)}) async-start(), calls=%async_computation.7 | async-start | bytes 327680 | tf_op jit(solution)/shard_map/reduce_scatter | solution.py:107
  211.7 15.1 %copy-start.1 = (bf16[384,32,128]{2,1,0:T(8,128)(2,1)S(1)}, bf16[384,32,128]{2,1,0:T(8,128)(2,1)}, u32[]{:S(2)}) copy-start(bf16[384,32,128]{2,1,0:T(8,128)(2,1)} %gather_fusion.1) | copy-start | bytes 9437188
  336.5 77.1 %reduce-scatter.7.cloned.1.call-start = ((), (), s32[]{:S(2)}) async-start(), calls=%async_computation.5 | async-start | bytes 327680 | tf_op jit(solution)/shard_map/reduce_scatter | solution.py:73
  339.2 9.3 copy-start.2
  384.2 10.5 copy-start.3
  394.7 649.0 %all-reduce.3.cloned.1.call-start = ((), (), s32[]{:S(2)}) async-start(), calls=%async_computation.8 | async-start | bytes 75497472 | tf_op jit(solution)/shard_map/psum | solution.py:123
  1043.7 12.6 %copy-start.5 = (bf16[1,1,384,128,128]{4,3,2,1,0:T(8,128)(2,1)S(1)}, bf16[1,1,384,128,128]{4,3,2,1,0:T(8,128)(2,1)}, u32[]{:S(2)}) copy-start(bf16[1,1,384,128,128]{4,3,2,1,0:T(8,128)(2,1)} %get-tuple-element.58) | copy-start | bytes 37748740
  1043.7 19.0 %slice-start = ((s8[12582912]{0:T(1024)(128)(4,1)}), s8[4194304]{0:T(1024)(128)(4,1)S(1)}, s32[]{:S(2)}) async-start(s8[12582912]{0:T(1024)(128)(4,1)} %bitcast.173), calls=%async_computation.9 | async-start | bytes 8388608
  1043.7 19.5 %slice-start.1 = ((s8[12582912]{0:T(1024)(128)(4,1)}), s8[4194304]{0:T(1024)(128)(4,1)S(1)}, s32[]{:S(2)}) async-start(s8[12582912]{0:T(1024)(128)(4,1)} %bitcast.173), calls=%async_computation.10 | async-start | bytes 8388608
  1056.3 8.6 slice-start.2
Sparse Core Ops, SparseCore 0:
  124.9 14.7 reduce-scatter.4
  190.5 11.3 reduce-scatter.8
  336.6 19.2 reduce-scatter.10
  394.8 18.7 reduce-scatter.6
  417.2 626.4 all-reduce.2
where the time goes:
time: 1090 us; the launch traced here: 1080 us
  waiting for transfers between devices  650 us (60%)
  other arithmetic  219 us (20%)
  matrix products  103 us (9%)
  blocking collectives  47.2 us (4%)
  local copies, waits for them, and re-layouts  43.4 us (4%)
  between operations  14.3 us (1%)
    psum x1, waiting for transfers between devices, on_device(): lax.psum(gate_part.astype(jnp.bfloat16), 'replica').astype(jnp.float32)  630 us
    scatter-add x6, other arithmetic, place_blocks(): placed = placed.at[:, index, :].add(product, mode='drop')  209 us
    unnamed x25, local copies, waits for them, and re-layouts  26 us
  transfers between devices with their start and end apart: 5, of which 3 were waited for; matrix products, arithmetic and copies ran while one was open for 11% of the time, Pallas kernels for 0%

commit v1 on v0

--- a/solution.py
+++ b/solution.py
@@ -120,7 +120,9 @@
         "tsk,tsf->skf", up_input, up_grad_picked, preferred_element_type=jnp.float32
     )
     gate_weight_grad, up_weight_grad, down_weight_grad = (
-        lax.psum(gate_part.astype(jnp.bfloat16), "replica").astype(jnp.float32),
+        jnp.sum(lax.all_gather(gate_part.astype(jnp.bfloat16), "replica"), axis=0).astype(
+            jnp.float32
+        ),
         lax.psum(up_part.astype(jnp.bfloat16), "replica").astype(jnp.float32),
         lax.psum(down_part.astype(jnp.bfloat16), "replica").astype(jnp.float32),
     )

time: 1090 us -> 1020 us (0.936)
  waiting for transfers between devices: 650 us -> 563 us
  other arithmetic: 219 us -> 244 us
    psum x1, waiting for transfers between devices: 630 us -> 425 us  [on_device(): lax.psum(up_part.astype(jnp.bfloat16), 'replica').astype(jnp.float32)]
    all_gather x0 -> x1, waiting for transfers between devices: none -> 108 us  [on_device(): lax.all_gather(gate_part.astype(jnp.bfloat16), 'replica')]
    reduce_sum x0 -> x1, other arithmetic: none -> 23.8 us  [on_device(): jnp.sum(lax.all_gather(gate_part.astype(jnp.bfloat16), 'replica'), axis=0)]
    reduce_scatter x1, waiting for transfers between devices: 0.02 us -> 19.3 us  [on_device(): lax.psum_scatter((place_blocks(gate_product, gate_rowslot, row_count, blo...]
    unnamed x25 -> x26, local copies, waits for them, and re-layouts: 26 us -> 18.5 us
  transfers between devices with their start and end apart: 5 -> 6, of which waited for: 3 -> 4; matrix products, arithmetic and copies ran while one was open for 11% -> 25% of each run, Pallas kernels for 0% -> 0%
where the time goes in v1:
time: 1020 us; the launch traced here: 1010 us
  waiting for transfers between devices  563 us (55%)
  other arithmetic  244 us (24%)
  matrix products  105 us (10%)
  blocking collectives  47 us (5%)
  local copies, waits for them, and re-layouts  35.1 us (3%)
  between operations  14.7 us (1%)
    psum x1, waiting for transfers between devices, on_device(): lax.psum(up_part.astype(jnp.bfloat16), 'replica').astype(jnp.float32)  425 us
    scatter-add x6, other arithmetic, place_blocks(): placed = placed.at[:, index, :].add(product, mode='drop')  210 us
    all_gather x1, waiting for transfers between devices, on_device(): lax.all_gather(gate_part.astype(jnp.bfloat16), 'replica')  108 us
    reduce_sum x1, other arithmetic, on_device(): jnp.sum(lax.all_gather(gate_part.astype(jnp.bfloat16), 'replica'), axis=0)  23.8 us
  transfers between devices with their start and end apart: 6, of which 4 were waited for; matrix products, arithmetic and copies ran while one was open for 25% of the time, Pallas kernels for 0%

profile of v1, /device:TPU:0, one launch (start us, length us, event | category | flops | bytes accessed | tf_op | source)
XLA Modules:
  0.0 1009.3 jit_solution(7164693377126411955)
XLA Ops:
  10.8 15.8 %all_gather.21 = bf16[32,4096]{1,0:T(8,128)(2,1)S(1)} all-gather(bf16[8,4096]{1,0:T(8,128)(2,1)} %param.12), channel_id=1, replica_groups=mesh['dp'=2,'tile'=4,'replica'=4] {'tile'}, dimensions={0}, use_global_device_ids=true | all-gather | bytes 327680 | tf_op jit(solution)/shard_map/all_gather | solution.py:33
  29.2 9.2 fusion.6
  38.5 34.8 %scatter_fusion.1 = f32[32,28,128]{2,0,1:T(8,128)S(1)} fusion(f32[32,28,128]{2,0,1:T(8,128)S(1)} %broadcast.390.clone.1, s32[384]{0:T(512)S(1)} %get-tuple-element.8, f32[384,32,128]{2,1,0:T(8,128)} %fusion.6), kind=kCustom, calls=%fused_computation.7 | custom fusion | flops 1572864 | bytes 18875904 | tf_op jit(solution)/shard_map/scatter-add | solution.py:23
  76.6 9.2 fusion.10
  85.9 34.9 %scatter_fusion = f32[32,28,128]{2,0,1:T(8,128)S(1)} fusion(f32[32,28,128]{2,0,1:T(8,128)S(1)} %broadcast.390.clone.2, s32[384]{0:T(512)S(1)} %get-tuple-element.14, f32[384,32,128]{2,1,0:T(8,128)} %fusion.10), kind=kCustom, calls=%fused_computation.6 | custom fusion | flops 1572864 | bytes 18875904 | tf_op jit(solution)/shard_map/scatter-add | solution.py:23
  121.8 14.3 %all_gather.23 = bf16[32,4096]{1,0:T(8,128)(2,1)S(1)} all-gather(bf16[8,4096]{1,0:T(8,128)(2,1)S(1)} %copy-done.9), channel_id=1, replica_groups=mesh['dp'=2,'tile'=4,'replica'=4] {'tile'}, dimensions={0}, use_global_device_ids=true | all-gather | bytes 327680 | tf_op jit(solution)/shard_map/all_gather | solution.py:34
  138.6 12.5 %fusion = f32[384,32,128]{2,1,0:T(8,128)} fusion(bf16[1,1,384,128,128]{4,3,2,1,0:T(8,128)(2,1)} %param.16, bf16[384,32,128]{2,1,0:T(8,128)(2,1)S(1)} %gather_fusion.3, pred[384]{0:T(512)(128)(4,1)S(1)} %get-tuple-element.25), kind=kOutput, calls=%fused_computation.12 | convolution fusion | flops 404226048 | bytes 22020480 | tf_op jit(solution)/shard_map/tsk,sfk->tsf/dot_general | solution.py:82
  151.1 34.9 %scatter_fusion.3 = f32[32,28,128]{2,0,1:T(8,128)S(1)} fusion(f32[32,28,128]{2,0,1:T(8,128)S(1)} %broadcast.390.clone, s32[384]{0:T(512)S(1)} %get-tuple-element.11, f32[384,32,128]{2,1,0:T(8,128)} %fusion), kind=kCustom, calls=%fused_computation.9 | custom fusion | flops 1572864 | bytes 18875904 | tf_op jit(solution)/shard_map/scatter-add | solution.py:23
  187.8 10.5 %reduce-scatter.9.cloned.1.call-done = bf16[16,3584]{1,0:T(8,128)(2,1)} async-done(((bf16[32,3584]{1,0:T(8,128)(2,1)}), bf16[16,3584]{1,0:T(8,128)(2,1)}) %reduce-scatter.9.cloned.1.call-update) | async-done | bytes 114704 | tf_op jit(solution)/shard_map/reduce_scatter | solution.py:85
  199.9 6.0 all_gather.24
  209.2 9.8 convolution_convert_fusion
  227.9 14.7 %fusion.2 = f32[384,32,128]{2,1,0:T(8,128)} fusion(bf16[1,1,384,128,128]{4,3,2,1,0:T(8,128)(2,1)} %param.16, bf16[384,32,128]{2,1,0:T(8,128)(2,1)S(1)} %gather_fusion.2, pred[384]{0:T(512)(128)(4,1)S(1)} %get-tuple-element.46), kind=kOutput, calls=%fused_computation.14 | convolution fusion | flops 404226048 | bytes 22020480 | tf_op jit(solution)/shard_map/tsf,sfk->tsk/dot_general | solution.py:70
  242.6 35.4 %scatter_fusion.2 = f32[32,32,128]{2,0,1:T(8,128)S(1)} fusion(f32[32,32,128]{2,0,1:T(8,128)S(1)} %broadcast.388.clone, s32[384]{0:T(512)S(1)} %get-tuple-element.12, f32[384,32,128]{2,1,0:T(8,128)} %fusion.2), kind=kCustom, calls=%fused_computation.8 | custom fusion | flops 1572864 | bytes 18875904 | tf_op jit(solution)/shard_map/scatter-add | solution.py:23
  283.5 14.9 %fusion.8 = f32[384,32,128]{2,1,0:T(8,128)} fusion(bf16[1,1,384,128,128]{4,3,2,1,0:T(8,128)(2,1)} %param.14, bf16[384,32,128]{2,1,0:T(8,128)(2,1)} %gather_fusion.4, pred[384]{0:T(512)(128)(4,1)S(1)} %get-tuple-element.23), kind=kOutput, calls=%fused_computation.20 | convolution fusion | flops 404226048 | bytes 22020480 | tf_op jit(solution)/shard_map/tsf,skf->tsk/dot_general | solution.py:103
  302.6 14.9 %fusion.4 = f32[384,32,128]{2,1,0:T(8,128)} fusion(bf16[1,1,384,128,128]{4,3,2,1,0:T(8,128)(2,1)} %param.15, bf16[384,32,128]{2,1,0:T(8,128)(2,1)} %gather_fusion.5, pred[384]{0:T(512)(128)(4,1)S(1)} %get-tuple-element.21), kind=kOutput, calls=%fused_computation.16 | convolution fusion | flops 404226048 | bytes 22020480 | tf_op jit(solution)/shard_map/tsf,skf->tsk/dot_general | solution.py:106
  317.6 34.9 %scatter_fusion.4 = f32[32,32,128]{2,0,1:T(8,128)S(1)} fusion(f32[32,32,128]{2,0,1:T(8,128)S(1)} %broadcast.388.clone.1, s32[384]{0:T(512)S(1)} %get-tuple-element.13, f32[384,32,128]{2,1,0:T(8,128)} %fusion.8), kind=kCustom, calls=%fused_computation.10 | custom fusion | flops 1572864 | bytes 18875904 | tf_op jit(solution)/shard_map/scatter-add | solution.py:23
  352.6 34.9 %scatter_fusion.5 = f32[32,32,128]{2,0,1:T(8,128)S(1)} fusion(f32[32,32,128]{2,0,1:T(8,128)S(1)} %broadcast.388.clone.2, s32[384]{0:T(512)S(1)} %get-tuple-element.7, f32[384,32,128]{2,1,0:T(8,128)} %fusion.4), kind=kCustom, calls=%fused_computation.11 | custom fusion | flops 1572864 | bytes 18875904 | tf_op jit(solution)/shard_map/scatter-add | solution.py:23
  388.2 10.4 %convert_bitcast_fusion.1 = bf16[1,1,384,128,128]{4,3,2,1,0:T(8,128)(2,1)} fusion(bf16[384,32,128]{2,1,0:T(8,128)(2,1)} %copy-done, pred[384]{0:T(512)(128)(4,1)S(1)} %get-tuple-element.42, bf16[384,32,128]{2,1,0:T(8,128)(2,1)} %gather_fusion.5, pred[384]{0:T(512)(128)(4,1)S(1)} %get-tuple-element.21), kind=kOutput, calls=%fused_computation.25 | convolution fusion | flops 412090368 | bytes 18875136 | tf_op jit(solution)/shard_map/tsk,tsf->skf/dot_general | solution.py:119
  399.0 9.7 convert_bitcast_fusion
  408.7 107.6 %all-gather.3.cloned.1.call-done = bf16[1536,128,128]{2,1,0:T(8,128)(2,1)} async-done(((bf16[384,128,128]{2,1,0:T(8,128)(2,1)}), bf16[1536,128,128]{2,1,0:T(8,128)(2,1)}) %all-gather.3.cloned.1.call-update) | async-done | bytes 50331664 | tf_op jit(solution)/shard_map/all_gather | solution.py:123
  516.3 23.8 %reduce_sum.12 = bf16[384,128,128]{2,1,0:T(8,128)(2,1)} reduce(bf16[4,384,128,128]{3,2,1,0:T(8,128)(2,1)} %bitcast.173, bf16[]{:T(256)} %constant.66.clone.1), dimensions={0}, to_apply=%region_10.13 | reduce | flops 18874368 | bytes 62914560 | tf_op jit(solution)/shard_map/reduce_sum | solution.py:123
  540.1 19.3 %reduce-scatter.11.cloned.1.call-done = bf16[8,4096]{1,0:T(8,128)(2,1)} async-done(((bf16[32,4096]{1,0:T(8,128)(2,1)}), bf16[8,4096]{1,0:T(8,128)(2,1)}) %reduce-scatter.11.cloned.1.call-update) | async-done | bytes 65552 | tf_op jit(solution)/shard_map/reduce_scatter | solution.py:107
  559.4 425.1 %all-reduce.3.cloned.1.call-done = (bf16[1,1,384,128,128]{4,3,2,1,0:T(8,128)(2,1)}, bf16[1,1,384,128,128]{4,3,2,1,0:T(8,128)(2,1)}) async-done(((bf16[1,1,384,128,128]{4,3,2,1,0:T(8,128)(2,1)}, bf16[1,1,384,128,128]{4,3,2,1,0:T(8,128)(2,1)}), (bf16[1,1,384,128,128]{4,3,2,1,0:T(8,128)(2,1)}, bf16[1,1,384,128,128]{4,3,2,1,0:T(8,128)(2,1)})) %all-reduce.3.cloned.1.call-update) | async-done | bytes 25165840 | tf_op jit(solution)/shard_map/psum | solution.py:126
  984.5 11.4 %copy.71 = bf16[1,1,384,128,128]{4,3,2,1,0:T(8,128)(2,1)} copy(bf16[1,1,384,128,128]{4,3,2,1,0:T(8,128)(2,1)} %get-tuple-element.57) | data formatting | bytes 25165824
  (83 shorter events, 45.5 us)
Async XLA Ops:
  7.2 179.7 %reduce-scatter.5.cloned.1.call-start = ((), (), s32[]{:S(2)}) async-start(), calls=%async_computation.4 | async-start | bytes 688128 | tf_op jit(solution)/shard_map/reduce_scatter | solution.py:50
  29.2 9.2 copy-start
  38.5 35.6 %copy-start.10 = (s32[1,1,384]{2,1,0:T(1,128)S(1)}, s32[1,1,384]{2,1,0:T(1,128)}, u32[]{:S(2)}) copy-start(s32[1,1,384]{2,1,0:T(1,128)} %param.17) | copy-start | bytes 4612
  76.5 9.3 copy-start.1
  85.8 35.0 %copy-start.7 = (bf16[32,3584]{1,0:T(8,128)(2,1)S(1)}, bf16[32,3584]{1,0:T(8,128)(2,1)}, u32[]{:S(2)}) copy-start(bf16[32,3584]{1,0:T(8,128)(2,1)} %copy_bitcast_fusion.5) | copy-start | bytes 688132
  85.9 35.8 %copy-start.11 = (s32[1,1,384]{2,1,0:T(1,128)S(1)}, s32[1,1,384]{2,1,0:T(1,128)}, u32[]{:S(2)}) copy-start(s32[1,1,384]{2,1,0:T(1,128)} %param.19) | copy-start | bytes 4612
  85.9 35.9 %copy-start.9 = (bf16[8,4096]{1,0:T(8,128)(2,1)S(1)}, bf16[8,4096]{1,0:T(8,128)(2,1)}, u32[]{:S(2)}) copy-start(bf16[8,4096]{1,0:T(8,128)(2,1)} %param.13) | copy-start | bytes 196612
  121.7 76.6 %reduce-scatter.9.cloned.1.call-start = ((), (), s32[]{:S(2)}) async-start(), calls=%async_computation.6 | async-start | bytes 344064 | tf_op jit(solution)/shard_map/reduce_scatter | solution.py:85
  138.5 12.5 %copy-start.5 = (bf16[384,32,128]{2,1,0:T(8,128)(2,1)}, bf16[384,32,128]{2,1,0:T(8,128)(2,1)S(1)}, u32[]{:S(2)}) copy-start(bf16[384,32,128]{2,1,0:T(8,128)(2,1)S(1)} %gather_fusion.3) | copy-start | bytes 9437188
  186.8 329.6 %all-gather.3.cloned.1.call-start = ((), (), s32[]{:S(2)}) async-start(), calls=%async_computation.8 | async-start | bytes 62914560 | tf_op jit(solution)/shard_map/all_gather | solution.py:123
  206.0 3.2 copy-start.2
  219.0 0.9 copy-start.8
  219.0 321.1 %reduce-scatter.7.cloned.1.call-start = ((), (), s32[]{:S(2)}) async-start(), calls=%async_computation.5 | async-start | bytes 327680 | tf_op jit(solution)/shard_map/reduce_scatter | solution.py:73
  227.8 14.7 %copy-start.3 = (bf16[384,32,128]{2,1,0:T(8,128)(2,1)}, bf16[384,32,128]{2,1,0:T(8,128)(2,1)S(1)}, u32[]{:S(2)}) copy-start(bf16[384,32,128]{2,1,0:T(8,128)(2,1)S(1)} %gather_fusion.2) | copy-start | bytes 9437188
  299.2 260.2 %reduce-scatter.11.cloned.1.call-start = ((), (), s32[]{:S(2)}) async-start(), calls=%async_computation.7 | async-start | bytes 327680 | tf_op jit(solution)/shard_map/reduce_scatter | solution.py:107
  388.2 10.7 %copy-start.4 = (bf16[384,32,128]{2,1,0:T(8,128)(2,1)S(1)}, bf16[384,32,128]{2,1,0:T(8,128)(2,1)}, u32[]{:S(2)}) copy-start(bf16[384,32,128]{2,1,0:T(8,128)(2,1)} %copy-done.3) | copy-start | bytes 9437188
  398.7 585.8 %all-reduce.3.cloned.1.call-start = ((), (), s32[]{:S(2)}) async-start(), calls=%async_computation.9 | async-start | bytes 50331648 | tf_op jit(solution)/shard_map/psum | solution.py:126
  984.5 12.9 %copy-start.6 = (bf16[1,1,384,128,128]{4,3,2,1,0:T(8,128)(2,1)S(1)}, bf16[1,1,384,128,128]{4,3,2,1,0:T(8,128)(2,1)}, u32[]{:S(2)}) copy-start(bf16[1,1,384,128,128]{4,3,2,1,0:T(8,128)(2,1)} %get-tuple-element.58) | copy-start | bytes 37748740
Sparse Core Ops, SparseCore 0:
  121.8 14.7 reduce-scatter.4
  186.9 11.3 reduce-scatter.8
  219.1 297.1 all-gather.2
  519.1 19.6 reduce-scatter.6
  541.5 17.9 reduce-scatter.10
  562.7 421.8 all-reduce.2
